TPU v7x, 32 devices: a whole 2x2x4 slice. The times are simulated.
32 devices in a mesh: gx: 4 (over x, core), gy: 8 (over z, y).
Axes of the slice: x: 2, y: 2, z: 4, core: 2. Of those that a mesh axis runs over, the one named last changes fastest.
Arguments:
- volume: bfloat16 [16, 64, 16, 128], P('gx', 'gy'), may hold values from -6 to 6
- basin_mask: int32 [16, 64, 32], P('gx', 'gy'), may hold values 0 or 1
- w_first: bfloat16 [27, 64, 128], replicated, may hold values from -0.15625 to 0.15625
- b_first: float32 [128], replicated, may hold values from -3 to 3
- w_second: bfloat16 [27, 128, 128], replicated, may hold values from -0.109375 to 0.109375
- b_second: float32 [128], replicated, may hold values from -3 to 3
- upstream: bfloat16 [16, 64, 32, 128], P('gx', 'gy'), may hold values from -6 to 6
Outputs:
- features: bfloat16 [16, 64, 32, 128], P('gx', 'gy')
- step_first: float32 [27, 64, 128], replicated
- step_second: float32 [27, 128, 128], replicated
Inputs may be any that keep to these rules, and one draw needn't show every extreme that they name: basin_mask holds only 0 and 1.
All inputs are finite; a program needn't handle non-finite values. No bound on the sum of `basin_mask` on one device may be relied on, other than what follows from the above.
Results may differ from a plain program's by a relative error of at most 0.0054.
Values may be sent and summed in bfloat16 or wider, within the bound.
No kernel may reach another device: no remote copies, remote signals or barrier semaphores. Data moves between devices by JAX's collectives and lax.ppermute only.
A program may use at most 64 MiB of HBM per device.

v0:
```python
import jax
import jax.numpy as jnp
from jax import lax
from jax.sharding import PartitionSpec as P


def extended_2(block, sides, width):
    for axis, dim in sides:
        count = lax.axis_size(axis)
        forward = [(i, i + 1) for i in range(count - 1)]
        backward = [(target, source) for source, target in forward]
        low = lax.ppermute(
            lax.slice_in_dim(block, block.shape[dim] - width, None, axis=dim), axis, forward
        )
        high = lax.ppermute(lax.slice_in_dim(block, 0, width, axis=dim), axis, backward)
        block = jnp.concatenate([low, block, high], axis=dim)
    return block


def pad_depth(extended):
    return jnp.pad(extended, ((0, 0), (0, 0), (1, 1), (0, 0)))


def group_window(padded, tap_x, tap_y, cells_x, cells_y, cells_z):
    parts = [
        padded[tap_x : tap_x + cells_x, tap_y : tap_y + cells_y, tap_z : tap_z + cells_z]
        for tap_z in range(3)
    ]
    joined = jnp.concatenate(parts, axis=-1)
    return joined.reshape(cells_x * cells_y * cells_z, joined.shape[3])


def convolve(padded, weights, cells_x, cells_y, cells_z):
    chan_in = weights.shape[1]
    total = jnp.zeros((cells_x * cells_y * cells_z, weights.shape[2]), jnp.float32)
    for tap_x in range(3):
        for tap_y in range(3):
            window = group_window(padded, tap_x, tap_y, cells_x, cells_y, cells_z)
            first = 9 * tap_x + 3 * tap_y
            kernel = weights[first : first + 3].reshape(3 * chan_in, weights.shape[2])
            total = total + jnp.dot(window, kernel, preferred_element_type=jnp.float32)
    return total


def weight_grad(padded, grad, cells_x, cells_y, cells_z):
    pieces = []
    for tap_x in range(3):
        for tap_y in range(3):
            window = group_window(padded, tap_x, tap_y, cells_x, cells_y, cells_z)
            product = lax.dot_general(
                window, grad, (((0,), (0,)), ((), ())), preferred_element_type=jnp.float32
            )
            pieces.append(product.reshape(3, padded.shape[3], grad.shape[1]))
    return jnp.concatenate(pieces, axis=0)


def normalized_with(grad, total, count):
    return grad * lax.rsqrt(total / count + 1e-06)


def on_device(volume, basin_mask, w_first, b_first, w_second, b_second, upstream):
    cells_x, cells_y, half_z, doubled = volume.shape
    chan_in = doubled // 2
    cells_z = 2 * half_z
    chan_out = w_first.shape[2]
    field = volume.reshape(cells_x, cells_y, cells_z, chan_in)
    active = basin_mask.astype(jnp.float32).reshape(-1, 1)
    padded_in = pad_depth(extended_2(field, (("gx", 0), ("gy", 1)), 1))
    pre_first = convolve(padded_in, w_first, cells_x, cells_y, cells_z) + b_first
    sig_first = jax.nn.sigmoid(pre_first)
    hidden = (
        (pre_first * sig_first * active)
        .astype(jnp.bfloat16)
        .reshape(cells_x, cells_y, cells_z, chan_out)
    )
    padded_hidden = pad_depth(extended_2(hidden, (("gx", 0), ("gy", 1)), 1))
    pre_second = convolve(padded_hidden, w_second, cells_x, cells_y, cells_z) + b_second
    sig_second = jax.nn.sigmoid(pre_second)
    features = (
        (pre_second * sig_second * active)
        .astype(jnp.bfloat16)
        .reshape(cells_x, cells_y, cells_z, chan_out)
    )
    grad_second = (
        upstream.reshape(-1, chan_out).astype(jnp.float32)
        * active
        * sig_second
        * (1.0 + pre_second * (1.0 - sig_second))
    ).astype(jnp.bfloat16)
    dw_second = weight_grad(padded_hidden, grad_second, cells_x, cells_y, cells_z)
    flipped = jnp.transpose(w_second[::-1], (0, 2, 1))
    grad_field = grad_second.reshape(cells_x, cells_y, cells_z, chan_out)
    padded_grad = pad_depth(extended_2(grad_field, (("gx", 0), ("gy", 1)), 1))
    back_hidden = convolve(padded_grad, flipped, cells_x, cells_y, cells_z)
    grad_first = (back_hidden * active * sig_first * (1.0 + pre_first * (1.0 - sig_first))).astype(
        jnp.bfloat16
    )
    dw_first = weight_grad(padded_in, grad_first, cells_x, cells_y, cells_z)
    count_first = float(dw_first.size)
    count_second = float(dw_second.size)
    sum_first, sum_second = lax.psum((dw_first, dw_second), ("gx", "gy"))
    step_first = normalized_with(sum_first, jnp.sum(sum_first * sum_first), count_first)
    step_second = normalized_with(sum_second, jnp.sum(sum_second * sum_second), count_second)
    return (features, step_first, step_second)


def solution(mesh):
    in_specs = (
        P("gx", "gy", None, None),
        P("gx", "gy", None),
        P(),
        P(),
        P(),
        P(),
        P("gx", "gy", None, None),
    )
    out_specs = (P("gx", "gy", None, None), P(), P())
    return jax.shard_map(
        on_device, mesh=mesh, in_specs=in_specs, out_specs=out_specs, check_vma=False
    )
```

profile of v0, /device:TPU:0, one launch (start us, length us, event | category | flops | bytes accessed | tf_op | source)
XLA Modules:
  0.0 280.9 jit_solution(11516559743100319684)
XLA Ops:
  8.2 2.4 collective-permute-start
  10.7 1.4 collective-permute-start.1
  12.1 2.2 fusion.62
  15.1 1.3 copy.31
  16.6 4.2 %collective-permute-start.2 = (bf16[6,1,32,64]{3,2,1,0:T(8,128)(2,1)S(1)}, bf16[6,1,32,64]{3,2,1,0:T(8,128)(2,1)S(1)}, u32[]{:S(2)}, u32[]{:S(2)}) collective-permute-start(bf16[6,1,32,64]{3,2,1,0:T(8,128)(2,1)S(1)} %get-tuple-element.116), channel_id=1, source_target_pairs={{0,1},{1,2},{2,3},{3,4},{4,5},{5,6},{6,7},{8,9},{9,10},{10,11},{11... | collective-permute-start | bytes 73736 | tf_op jit(solution)/shard_map/ppermute | solution.py:12
  20.8 1.3 collective-permute-start.3
  24.0 2.9 %collective-permute-done.3 = bf16[6,1,32,64]{3,2,1,0:T(8,128)(2,1)S(1)} collective-permute-done((bf16[6,1,32,64]{3,2,1,0:T(8,128)(2,1)S(1)}, bf16[6,1,32,64]{3,2,1,0:T(8,128)(2,1)S(1)}, u32[]{:S(2)}, u32[]{:S(2)}) %collective-permute-start.3) | collective-permute-done | bytes 24608 | tf_op jit(solution)/shard_map/ppermute | solution.py:15
  32.9 1.1 multiply_convert_fusion.1
  34.0 3.0 %collective-permute-start.4 = (bf16[1,8,32,128]{3,2,1,0:T(8,128)(2,1)S(1)}, bf16[1,8,32,128]{3,2,1,0:T(8,128)(2,1)S(1)}, u32[]{:S(2)}, u32[]{:S(2)}) collective-permute-start(bf16[1,8,32,128]{3,2,1,0:T(8,128)(2,1)S(1)} %bitcast.334), channel_id=1, source_target_pairs={{0,8},{8,16},{16,24},{1,9},{9,17},{17,25},{2,10},{10,18},{18,26},{... | collective-permute-start | bytes 196616 | tf_op jit(solution)/shard_map/ppermute | solution.py:12
  37.0 1.3 collective-permute-start.5
  39.3 3.5 %collective-permute-done.5 = bf16[1,8,32,128]{3,2,1,0:T(8,128)(2,1)S(1)} collective-permute-done((bf16[1,8,32,128]{3,2,1,0:T(8,128)(2,1)S(1)}, bf16[1,8,32,128]{3,2,1,0:T(8,128)(2,1)S(1)}, u32[]{:S(2)}, u32[]{:S(2)}) %collective-permute-start.5) | collective-permute-done | bytes 65568 | tf_op jit(solution)/shard_map/ppermute | solution.py:15
  43.5 5.0 %collective-permute-start.6 = (bf16[6,1,32,128]{3,2,1,0:T(8,128)(2,1)}, bf16[6,1,32,128]{3,2,1,0:T(8,128)(2,1)}, u32[]{:S(2)}, u32[]{:S(2)}) collective-permute-start(bf16[6,1,32,128]{3,2,1,0:T(8,128)(2,1)} %get-tuple-element.110), channel_id=1, source_target_pairs={{0,1},{1,2},{2,3},{3,4},{4,5},{5,6},{6,7},{8,9},{9,10},{10,11},{11... | collective-permute-start | bytes 147464 | tf_op jit(solution)/shard_map/ppermute | solution.py:12
  48.4 1.5 collective-permute-start.7
  49.9 1.0 fusion.57
  51.0 2.0 copy.30
  62.5 1.1 select_maximum_fusion.4
  63.6 1.7 fusion.64
  66.4 1.2 copy.40
  67.6 2.1 fusion.76
  69.6 1.1 fusion.14
  70.7 1.2 copy.41
  72.0 1.2 copy.42
  73.2 1.1 pad_maximum_fusion.6
  74.4 1.2 copy.43
  75.7 1.2 copy.45
  76.8 1.2 pad_maximum_fusion.9
  78.1 1.2 copy.46
  79.3 2.3 copy.47
  81.6 1.7 convolution_add_fusion.15
  87.6 1.3 fusion.42
  89.5 1.0 convolution_dynamic-update-slice_fusion.8
  90.6 1.2 copy.44
  91.7 4.7 %collective-permute-start.8 = (bf16[1,8,32,128]{3,2,1,0:T(8,128)(2,1)}, bf16[1,8,32,128]{3,2,1,0:T(8,128)(2,1)S(1)}, u32[]{:S(2)}, u32[]{:S(2)}) collective-permute-start(bf16[1,8,32,128]{3,2,1,0:T(8,128)(2,1)} %bitcast.45), channel_id=1, source_target_pairs={{0,8},{8,16},{16,24},{1,9},{9,17},{17,25},{2,10},{10,18},{18,26},{... | collective-permute-start | bytes 196616 | tf_op jit(solution)/shard_map/ppermute | solution.py:12
  96.4 1.5 collective-permute-start.9
  98.0 1.1 convolution_dynamic-update-slice_fusion.7
  99.0 1.0 convolution_dynamic-update-slice_fusion.6
  100.1 1.0 convolution_dynamic-update-slice_fusion.5
  101.1 1.1 convolution_dynamic-update-slice_fusion.4
  102.2 1.0 convolution_dynamic-update-slice_fusion.3
  103.2 1.1 convolution_dynamic-update-slice_fusion.2
  104.3 1.0 convolution_dynamic-update-slice_fusion.1
  105.7 4.3 %collective-permute-start.10 = (bf16[6,1,32,128]{3,2,1,0:T(8,128)(2,1)S(1)}, bf16[6,1,32,128]{3,2,1,0:T(8,128)(2,1)S(1)}, u32[]{:S(2)}, u32[]{:S(2)}) collective-permute-start(bf16[6,1,32,128]{3,2,1,0:T(8,128)(2,1)S(1)} %get-tuple-element.106), channel_id=1, source_target_pairs={{0,1},{1,2},{2,3},{3,4},{4,5},{5,6},{6,7},{8,9},{9,10},{10,11},{11... | collective-permute-start | bytes 147464 | tf_op jit(solution)/shard_map/ppermute | solution.py:12
  110.0 1.3 collective-permute-start.11
  111.3 1.1 convolution_dynamic-update-slice_fusion
  112.3 4.1 %collective-permute-done.11 = bf16[6,1,32,128]{3,2,1,0:T(8,128)(2,1)S(1)} collective-permute-done((bf16[6,1,32,128]{3,2,1,0:T(8,128)(2,1)S(1)}, bf16[6,1,32,128]{3,2,1,0:T(8,128)(2,1)S(1)}, u32[]{:S(2)}, u32[]{:S(2)}) %collective-permute-start.11) | collective-permute-done | bytes 49184 | tf_op jit(solution)/shard_map/ppermute | solution.py:15
  128.5 138.2 %all-reduce.6.cloned.1.call-done = (f32[27,64,128]{2,1,0:T(8,128)}, f32[27,128,128]{2,1,0:T(8,128)}) async-done(((f32[27,64,128]{2,1,0:T(8,128)}, f32[27,128,128]{2,1,0:T(8,128)}), (f32[27,64,128]{2,1,0:T(8,128)}, f32[27,128,128]{2,1,0:T(8,128)})) %all-reduce.6.cloned.1.call-update) | async-done | bytes 2654224 | tf_op jit(solution)/shard_map/psum | solution.py:101
  266.7 2.7 multiply_reduce_fusion
  270.1 1.3 broadcast_multiply_fusion
  (226 shorter events, 40.8 us)
Async XLA Ops:
  7.2 7.8 %copy-start.37 = (bf16[4,8,16,128]{3,2,1,0:T(8,128)(2,1)S(1)}, bf16[4,8,16,128]{3,2,1,0:T(8,128)(2,1)}, u32[]{:S(2)}) copy-start(bf16[4,8,16,128]{3,2,1,0:T(8,128)(2,1)} %param.7) | copy-start | bytes 393220
  7.2 7.1 %copy-start.38 = (bf16[27,64,128]{2,1,0:T(8,128)(2,1)S(1)}, bf16[27,64,128]{2,1,0:T(8,128)(2,1)}, u32[]{:S(2)}) copy-start(bf16[27,64,128]{2,1,0:T(8,128)(2,1)} %param.9) | copy-start | bytes 1327108
  7.2 259.5 %all-reduce.6.cloned.1.call-start = ((), (), s32[]{:S(2)}) async-start(), calls=%async_computation | async-start | bytes 5308416 | tf_op jit(solution)/shard_map/psum | solution.py:101
  8.2 8.3 %collective-permute-start = (bf16[1,8,32,64]{3,2,1,0:T(8,128)(2,1)S(1)}, bf16[1,8,32,64]{3,2,1,0:T(8,128)(2,1)S(1)}, u32[]{:S(2)}, u32[]{:S(2)}) collective-permute-start(bf16[1,8,32,64]{3,2,1,0:T(8,128)(2,1)S(1)} %slice.487), channel_id=1, source_target_pairs={{0,8},{8,16},{16,24},{1,9},{9,17},{17,25},{2,10},{10,18},{18,26},{... | collective-permute-start | bytes 98312 | tf_op jit(solution)/shard_map/ppermute | solution.py:12
  10.6 4.6 %copy-start.4 = (bf16[27,128,128]{2,1,0:T(8,128)(2,1)S(1)}, bf16[27,128,128]{2,1,0:T(8,128)(2,1)}, u32[]{:S(2)}) copy-start(bf16[27,128,128]{2,1,0:T(8,128)(2,1)} %param.11) | copy-start | bytes 2654212
  10.7 5.9 %collective-permute-start.1 = (bf16[1,8,32,64]{3,2,1,0:T(8,128)(2,1)S(1)}, bf16[1,8,32,64]{3,2,1,0:T(8,128)(2,1)S(1)}, u32[]{:S(2)}, u32[]{:S(2)}) collective-permute-start(bf16[1,8,32,64]{3,2,1,0:T(8,128)(2,1)S(1)} %slice.489), channel_id=1, source_target_pairs={{8,0},{16,8},{24,16},{9,1},{17,9},{25,17},{10,2},{18,10},{26,18},{... | collective-permute-start | bytes 98312 | tf_op jit(solution)/shard_map/ppermute | solution.py:15
  16.5 6.8 %copy-start.58 = (s32[4,8,32]{2,1,0:T(8,128)S(1)}, s32[4,8,32]{2,1,0:T(8,128)}, u32[]{:S(2)}) copy-start(s32[4,8,32]{2,1,0:T(8,128)} %param.8) | copy-start | bytes 12292
  16.6 7.4 %collective-permute-start.2 = (bf16[6,1,32,64]{3,2,1,0:T(8,128)(2,1)S(1)}, bf16[6,1,32,64]{3,2,1,0:T(8,128)(2,1)S(1)}, u32[]{:S(2)}, u32[]{:S(2)}) collective-permute-start(bf16[6,1,32,64]{3,2,1,0:T(8,128)(2,1)S(1)} %get-tuple-element.116), channel_id=1, source_target_pairs={{0,1},{1,2},{2,3},{3,4},{4,5},{5,6},{6,7},{8,9},{9,10},{10,11},{11... | collective-permute-start | bytes 73736 | tf_op jit(solution)/shard_map/ppermute | solution.py:12
  20.8 6.0 %collective-permute-start.3 = (bf16[6,1,32,64]{3,2,1,0:T(8,128)(2,1)S(1)}, bf16[6,1,32,64]{3,2,1,0:T(8,128)(2,1)S(1)}, u32[]{:S(2)}, u32[]{:S(2)}) collective-permute-start(bf16[6,1,32,64]{3,2,1,0:T(8,128)(2,1)S(1)} %get-tuple-element.117), channel_id=1, source_target_pairs={{1,0},{2,1},{3,2},{4,3},{5,4},{6,5},{7,6},{9,8},{10,9},{11,10},{12... | collective-permute-start | bytes 73736 | tf_op jit(solution)/shard_map/ppermute | solution.py:15
  23.3 8.1 %copy-start.15 = (bf16[1024,64]{1,0:T(8,128)(2,1)}, bf16[1024,64]{1,0:T(8,128)(2,1)S(1)}, u32[]{:S(2)}) copy-start(bf16[1024,64]{1,0:T(8,128)(2,1)S(1)} %concatenate.198) | copy-start | bytes 393220
  28.4 1.3 copy-start.3
  29.7 3.0 %copy-start.17 = (bf16[4,8,32,192]{3,2,1,0:T(8,128)(2,1)}, bf16[4,8,32,192]{3,2,1,0:T(8,128)(2,1)S(1)}, u32[]{:S(2)}) copy-start(bf16[4,8,32,192]{3,2,1,0:T(8,128)(2,1)S(1)} %get-tuple-element.112) | copy-start | bytes 1179652
  32.9 5.5 %copy-start.5 = (bf16[27,128,128]{2,1,0:T(8,128)(2,1)S(1)}, bf16[27,128,128]{2,1,0:T(8,128)(2,1)}, u32[]{:S(2)}) copy-start(bf16[27,128,128]{2,1,0:T(8,128)(2,1)} %reverse_bitcast_fusion) | copy-start | bytes 2654212
  34.0 15.9 %copy-start.16 = (bf16[1024,64]{1,0:T(8,128)(2,1)S(1)}, bf16[1024,64]{1,0:T(8,128)(2,1)}, u32[]{:S(2)}) copy-start(bf16[1024,64]{1,0:T(8,128)(2,1)} %copy-done.15) | copy-start | bytes 393220
  34.0 5.3 %collective-permute-start.4 = (bf16[1,8,32,128]{3,2,1,0:T(8,128)(2,1)S(1)}, bf16[1,8,32,128]{3,2,1,0:T(8,128)(2,1)S(1)}, u32[]{:S(2)}, u32[]{:S(2)}) collective-permute-start(bf16[1,8,32,128]{3,2,1,0:T(8,128)(2,1)S(1)} %bitcast.334), channel_id=1, source_target_pairs={{0,8},{8,16},{16,24},{1,9},{9,17},{17,25},{2,10},{10,18},{18,26},{... | collective-permute-start | bytes 196616 | tf_op jit(solution)/shard_map/ppermute | solution.py:12
  37.0 5.8 %collective-permute-start.5 = (bf16[1,8,32,128]{3,2,1,0:T(8,128)(2,1)S(1)}, bf16[1,8,32,128]{3,2,1,0:T(8,128)(2,1)S(1)}, u32[]{:S(2)}, u32[]{:S(2)}) collective-permute-start(bf16[1,8,32,128]{3,2,1,0:T(8,128)(2,1)S(1)} %bitcast.333), channel_id=1, source_target_pairs={{8,0},{16,8},{24,16},{9,1},{17,9},{25,17},{10,2},{18,10},{26,18},{... | collective-permute-start | bytes 196616 | tf_op jit(solution)/shard_map/ppermute | solution.py:15
  43.5 17.2 %collective-permute-start.6 = (bf16[6,1,32,128]{3,2,1,0:T(8,128)(2,1)}, bf16[6,1,32,128]{3,2,1,0:T(8,128)(2,1)}, u32[]{:S(2)}, u32[]{:S(2)}) collective-permute-start(bf16[6,1,32,128]{3,2,1,0:T(8,128)(2,1)} %get-tuple-element.110), channel_id=1, source_target_pairs={{0,1},{1,2},{2,3},{3,4},{4,5},{5,6},{6,7},{8,9},{9,10},{10,11},{11... | collective-permute-start | bytes 147464 | tf_op jit(solution)/shard_map/ppermute | solution.py:12
  48.4 12.2 %collective-permute-start.7 = (bf16[6,1,32,128]{3,2,1,0:T(8,128)(2,1)}, bf16[6,1,32,128]{3,2,1,0:T(8,128)(2,1)}, u32[]{:S(2)}, u32[]{:S(2)}) collective-permute-start(bf16[6,1,32,128]{3,2,1,0:T(8,128)(2,1)} %get-tuple-element.111), channel_id=1, source_target_pairs={{1,0},{2,1},{3,2},{4,3},{5,4},{6,5},{7,6},{9,8},{10,9},{11,10},{12... | collective-permute-start | bytes 147464 | tf_op jit(solution)/shard_map/ppermute | solution.py:15
  54.0 1.9 copy-start.19
  56.9 2.8 %copy-start.18 = (bf16[4,8,32,192]{3,2,1,0:T(8,128)(2,1)S(1)}, bf16[4,8,32,192]{3,2,1,0:T(8,128)(2,1)}, u32[]{:S(2)}) copy-start(bf16[4,8,32,192]{3,2,1,0:T(8,128)(2,1)} %copy-done.17) | copy-start | bytes 1179652
  70.7 1.3 copy-start.2
  71.9 1.3 copy-start.34
  74.4 1.2 copy-start.36
  79.3 4.1 %copy-start.49 = (bf16[3,128,128]{2,1,0:T(8,128)(2,1)S(1)}, bf16[3,128,128]{2,1,0:T(8,128)(2,1)}, u32[]{:S(2)}) copy-start(bf16[3,128,128]{2,1,0:T(8,128)(2,1)} %get-tuple-element.20) | copy-start | bytes 294916
  81.6 2.1 copy-start.48
  85.4 1.1 copy-start.1
  85.4 1.1 copy-start.43
  86.0 1.2 copy-start.35
  87.6 1.9 copy-start.7
  88.8 9.1 %copy-start.8 = (bf16[1024,384]{0,1:T(8,128)(2,1)S(1)}, bf16[1024,384]{0,1:T(8,128)(2,1)}, u32[]{:S(2)}) copy-start(bf16[1024,384]{0,1:T(8,128)(2,1)} %copy.41) | copy-start | bytes 2359300
  90.6 8.5 %copy-start.9 = (bf16[1024,384]{0,1:T(8,128)(2,1)S(1)}, bf16[1024,384]{0,1:T(8,128)(2,1)}, u32[]{:S(2)}) copy-start(bf16[1024,384]{0,1:T(8,128)(2,1)} %copy.42) | copy-start | bytes 2359300
  91.7 8.3 %copy-start.11 = (bf16[1024,384]{0,1:T(8,128)(2,1)S(1)}, bf16[1024,384]{0,1:T(8,128)(2,1)}, u32[]{:S(2)}) copy-start(bf16[1024,384]{0,1:T(8,128)(2,1)} %copy.43) | copy-start | bytes 2359300
  91.7 13.9 %collective-permute-start.8 = (bf16[1,8,32,128]{3,2,1,0:T(8,128)(2,1)}, bf16[1,8,32,128]{3,2,1,0:T(8,128)(2,1)S(1)}, u32[]{:S(2)}, u32[]{:S(2)}) collective-permute-start(bf16[1,8,32,128]{3,2,1,0:T(8,128)(2,1)} %bitcast.45), channel_id=1, source_target_pairs={{0,8},{8,16},{16,24},{1,9},{9,17},{17,25},{2,10},{10,18},{18,26},{... | collective-permute-start | bytes 196616 | tf_op jit(solution)/shard_map/ppermute | solution.py:12
  96.4 9.2 %collective-permute-start.9 = (bf16[1,8,32,128]{3,2,1,0:T(8,128)(2,1)}, bf16[1,8,32,128]{3,2,1,0:T(8,128)(2,1)S(1)}, u32[]{:S(2)}, u32[]{:S(2)}) collective-permute-start(bf16[1,8,32,128]{3,2,1,0:T(8,128)(2,1)} %bitcast.332), channel_id=1, source_target_pairs={{8,0},{16,8},{24,16},{9,1},{17,9},{25,17},{10,2},{18,10},{26,18},{... | collective-permute-start | bytes 196616 | tf_op jit(solution)/shard_map/ppermute | solution.py:15
  98.0 3.2 %copy-start.14 = (bf16[384,1024]{1,0:T(8,128)(2,1)S(1)}, bf16[384,1024]{1,0:T(8,128)(2,1)}, u32[]{:S(2)}) copy-start(bf16[384,1024]{1,0:T(8,128)(2,1)} %copy.44) | copy-start | bytes 2359300
  99.0 3.2 %copy-start.10 = (bf16[1024,384]{0,1:T(8,128)(2,1)S(1)}, bf16[1024,384]{0,1:T(8,128)(2,1)}, u32[]{:S(2)}) copy-start(bf16[1024,384]{0,1:T(8,128)(2,1)} %copy.45) | copy-start | bytes 2359300
  100.1 3.2 %copy-start.13 = (bf16[1024,384]{0,1:T(8,128)(2,1)S(1)}, bf16[1024,384]{0,1:T(8,128)(2,1)}, u32[]{:S(2)}) copy-start(bf16[1024,384]{0,1:T(8,128)(2,1)} %copy.46) | copy-start | bytes 2359300
  101.1 3.2 %copy-start.12 = (bf16[1024,384]{0,1:T(8,128)(2,1)S(1)}, bf16[1024,384]{0,1:T(8,128)(2,1)}, u32[]{:S(2)}) copy-start(bf16[1024,384]{0,1:T(8,128)(2,1)} %copy.47) | copy-start | bytes 2359300
  105.7 6.6 %collective-permute-start.10 = (bf16[6,1,32,128]{3,2,1,0:T(8,128)(2,1)S(1)}, bf16[6,1,32,128]{3,2,1,0:T(8,128)(2,1)S(1)}, u32[]{:S(2)}, u32[]{:S(2)}) collective-permute-start(bf16[6,1,32,128]{3,2,1,0:T(8,128)(2,1)S(1)} %get-tuple-element.106), channel_id=1, source_target_pairs={{0,1},{1,2},{2,3},{3,4},{4,5},{5,6},{6,7},{8,9},{9,10},{10,11},{11... | collective-permute-start | bytes 147464 | tf_op jit(solution)/shard_map/ppermute | solution.py:12
  110.0 6.4 %collective-permute-start.11 = (bf16[6,1,32,128]{3,2,1,0:T(8,128)(2,1)S(1)}, bf16[6,1,32,128]{3,2,1,0:T(8,128)(2,1)S(1)}, u32[]{:S(2)}, u32[]{:S(2)}) collective-permute-start(bf16[6,1,32,128]{3,2,1,0:T(8,128)(2,1)S(1)} %get-tuple-element.107), channel_id=1, source_target_pairs={{1,0},{2,1},{3,2},{4,3},{5,4},{6,5},{7,6},{9,8},{10,9},{11,10},{12... | collective-permute-start | bytes 147464 | tf_op jit(solution)/shard_map/ppermute | solution.py:15
  124.1 1.3 copy-start.28
  124.6 1.4 copy-start.25
  124.6 1.6 copy-start.24
  125.4 1.1 copy-start.23
  125.7 1.1 copy-start.22
  125.9 1.1 copy-start.21
  266.7 3.4 %copy-start = (f32[27,128,128]{2,1,0:T(8,128)S(1)}, f32[27,128,128]{2,1,0:T(8,128)}, u32[]{:S(2)}) copy-start(f32[27,128,128]{2,1,0:T(8,128)} %get-tuple-element.4) | copy-start | bytes 5308420
  270.1 1.5 copy-start.6
  (29 other events, 27.6 us)
Sparse Core Ops, SparseCore 0:
  128.7 138.0 all-reduce.5
where the time goes:
time: 282 us; the launch traced here: 281 us
  waiting for transfers between devices  149 us (53%)
  local copies, waits for them, and re-layouts  40.8 us (14%)
  starting transfers between devices  31.9 us (11%)
  matrix products  25.8 us (9%)
  other arithmetic  17.3 us (6%)
  between operations  16.5 us (6%)
    psum x1, waiting for transfers between devices, on_device(): sum_first, sum_second = lax.psum((dw_first, dw_second), ('gx', 'gy'))  138 us
    ppermute x6, starting transfers between devices, extended_2(): lax.ppermute(lax.slice_in_dim(block, block.shape[dim] - width, None, axis...  23.6 us
    dot_general x27, matrix products, convolve(): total = total + jnp.dot(window, kernel, preferred_element_type=jnp.float32)  14.1 us
    dot_general x18, matrix products, weight_grad(): lax.dot_general(window, grad, (((0,), (0,)), ((), ())), preferred_element...  11.8 us
    dot_general x10, local copies, waits for them, and re-layouts, weight_grad(): lax.dot_general(window, grad, (((0,), (0,)), ((), ())), preferred_element...  10.8 us
    ppermute x6, waiting for transfers between devices, extended_2(): lax.ppermute(lax.slice_in_dim(block, 0, width, axis=dim), axis, backward)  10.4 us
    reshape x8, local copies, waits for them, and re-layouts, group_window(): return joined.reshape(cells_x * cells_y * cells_z, joined.shape[3])  9.72 us
    ppermute x6, starting transfers between devices, extended_2(): lax.ppermute(lax.slice_in_dim(block, 0, width, axis=dim), axis, backward)  8.27 us
  transfers between devices with their start and end apart: 13, of which 4 were waited for; matrix products, arithmetic and copies ran while one was open for 9% of the time, Pallas kernels for 0%

commit v1 on v0

--- a/solution.py
+++ b/solution.py
@@ -98,7 +98,7 @@
     dw_first = weight_grad(padded_in, grad_first, cells_x, cells_y, cells_z)
     count_first = float(dw_first.size)
     count_second = float(dw_second.size)
-    sum_first, sum_second = lax.psum((dw_first, dw_second), ("gx", "gy"))
+    sum_first, sum_second = lax.psum(lax.psum((dw_first, dw_second), "gy"), "gx")
     step_first = normalized_with(sum_first, jnp.sum(sum_first * sum_first), count_first)
     step_second = normalized_with(sum_second, jnp.sum(sum_second * sum_second), count_second)
     return (features, step_first, step_second)

time: 282 us -> 324 us (1.15)
  waiting for transfers between devices: 149 us -> 190 us
    psum x1 -> x2, waiting for transfers between devices: 138 us -> 180 us  [the longest x1 118 us: on_device(): lax.psum((dw_first, dw_second), 'gy')]
  transfers between devices with their start and end apart: 13 -> 14, of which waited for: 4 -> 5; matrix products, arithmetic and copies ran while one was open for 9% -> 8% of each run, Pallas kernels for 0% -> 0%
where the time goes in v1:
time: 324 us; the launch traced here: 322 us
  waiting for transfers between devices  190 us (59%)
  local copies, waits for them, and re-layouts  40.8 us (13%)
  starting transfers between devices  31.9 us (10%)
  matrix products  25.9 us (8%)
  other arithmetic  17.2 us (5%)
  between operations  16.5 us (5%)
    psum x1, waiting for transfers between devices, on_device(): lax.psum((dw_first, dw_second), 'gy')  118 us
    psum x1, waiting for transfers between devices, on_device(): lax.psum(lax.psum((dw_first, dw_second), 'gy'), 'gx')  61.9 us
    ppermute x6, starting transfers between devices, extended_2(): lax.ppermute(lax.slice_in_dim(block, block.shape[dim] - width, None, axis...  23.5 us
    dot_general x27, matrix products, convolve(): total = total + jnp.dot(window, kernel, preferred_element_type=jnp.float32)  14.1 us
    dot_general x18, matrix products, weight_grad(): lax.dot_general(window, grad, (((0,), (0,)), ((), ())), preferred_element...  11.8 us
    dot_general x10, local copies, waits for them, and re-layouts, weight_grad(): lax.dot_general(window, grad, (((0,), (0,)), ((), ())), preferred_element...  10.8 us
    ppermute x6, waiting for transfers between devices, extended_2(): lax.ppermute(lax.slice_in_dim(block, 0, width, axis=dim), axis, backward)  10.4 us
    reshape x8, local copies, waits for them, and re-layouts, group_window(): return joined.reshape(cells_x * cells_y * cells_z, joined.shape[3])  9.72 us
  transfers between devices with their start and end apart: 14, of which 5 were waited for; matrix products, arithmetic and copies ran while one was open for 8% of the time, Pallas kernels for 0%

profile of v1, /device:TPU:0, one launch (start us, length us, event | category | flops | bytes accessed | tf_op | source)
XLA Modules:
  0.0 322.4 jit_solution(13862556347170446722)
XLA Ops:
  8.2 2.4 collective-permute-start
  10.7 1.4 collective-permute-start.1
  12.1 2.2 fusion.62
  15.2 1.3 copy.31
  16.6 4.2 %collective-permute-start.2 = (bf16[6,1,32,64]{3,2,1,0:T(8,128)(2,1)S(1)}, bf16[6,1,32,64]{3,2,1,0:T(8,128)(2,1)S(1)}, u32[]{:S(2)}, u32[]{:S(2)}) collective-permute-start(bf16[6,1,32,64]{3,2,1,0:T(8,128)(2,1)S(1)} %get-tuple-element.118), channel_id=1, source_target_pairs={{0,1},{1,2},{2,3},{3,4},{4,5},{5,6},{6,7},{8,9},{9,10},{10,11},{11... | collective-permute-start | bytes 73736 | tf_op jit(solution)/shard_map/ppermute | solution.py:12
  20.9 1.3 collective-permute-start.3
  24.0 2.8 collective-permute-done.3
  32.9 1.1 multiply_convert_fusion.1
  34.0 3.0 collective-permute-start.4
  37.1 1.3 collective-permute-start.5
  39.4 3.5 %collective-permute-done.5 = bf16[1,8,32,128]{3,2,1,0:T(8,128)(2,1)S(1)} collective-permute-done((bf16[1,8,32,128]{3,2,1,0:T(8,128)(2,1)S(1)}, bf16[1,8,32,128]{3,2,1,0:T(8,128)(2,1)S(1)}, u32[]{:S(2)}, u32[]{:S(2)}) %collective-permute-start.5) | collective-permute-done | bytes 65568 | tf_op jit(solution)/shard_map/ppermute | solution.py:15
  43.5 4.9 %collective-permute-start.6 = (bf16[6,1,32,128]{3,2,1,0:T(8,128)(2,1)}, bf16[6,1,32,128]{3,2,1,0:T(8,128)(2,1)}, u32[]{:S(2)}, u32[]{:S(2)}) collective-permute-start(bf16[6,1,32,128]{3,2,1,0:T(8,128)(2,1)} %get-tuple-element.112), channel_id=1, source_target_pairs={{0,1},{1,2},{2,3},{3,4},{4,5},{5,6},{6,7},{8,9},{9,10},{10,11},{11... | collective-permute-start | bytes 147464 | tf_op jit(solution)/shard_map/ppermute | solution.py:12
  48.5 1.5 collective-permute-start.7
  51.0 2.0 copy.30
  62.5 1.1 select_maximum_fusion.4
  63.6 1.7 fusion.64
  66.3 1.2 copy.40
  67.5 2.1 fusion.76
  69.6 1.1 fusion.14
  70.7 1.2 copy.41
  72.0 1.2 copy.42
  73.2 1.1 pad_maximum_fusion.6
  74.3 1.2 copy.43
  75.6 1.2 copy.45
  76.8 1.2 pad_maximum_fusion.9
  78.1 1.2 copy.46
  79.3 2.3 copy.47
  81.6 1.7 convolution_add_fusion.15
  87.6 1.2 fusion.42
  89.4 1.0 convolution_dynamic-update-slice_fusion.8
  90.5 1.2 copy.44
  91.7 4.7 %collective-permute-start.8 = (bf16[1,8,32,128]{3,2,1,0:T(8,128)(2,1)}, bf16[1,8,32,128]{3,2,1,0:T(8,128)(2,1)S(1)}, u32[]{:S(2)}, u32[]{:S(2)}) collective-permute-start(bf16[1,8,32,128]{3,2,1,0:T(8,128)(2,1)} %bitcast.45), channel_id=1, source_target_pairs={{0,8},{8,16},{16,24},{1,9},{9,17},{17,25},{2,10},{10,18},{18,26},{... | collective-permute-start | bytes 196616 | tf_op jit(solution)/shard_map/ppermute | solution.py:12
  96.4 1.5 collective-permute-start.9
  97.9 1.1 convolution_dynamic-update-slice_fusion.7
  99.0 1.0 convolution_dynamic-update-slice_fusion.6
  100.0 1.0 convolution_dynamic-update-slice_fusion.5
  101.1 1.1 convolution_dynamic-update-slice_fusion.4
  102.1 1.0 convolution_dynamic-update-slice_fusion.3
  103.2 1.1 convolution_dynamic-update-slice_fusion.2
  104.2 1.0 convolution_dynamic-update-slice_fusion.1
  105.6 4.3 %collective-permute-start.10 = (bf16[6,1,32,128]{3,2,1,0:T(8,128)(2,1)S(1)}, bf16[6,1,32,128]{3,2,1,0:T(8,128)(2,1)S(1)}, u32[]{:S(2)}, u32[]{:S(2)}) collective-permute-start(bf16[6,1,32,128]{3,2,1,0:T(8,128)(2,1)S(1)} %get-tuple-element.108), channel_id=1, source_target_pairs={{0,1},{1,2},{2,3},{3,4},{4,5},{5,6},{6,7},{8,9},{9,10},{10,11},{11... | collective-permute-start | bytes 147464 | tf_op jit(solution)/shard_map/ppermute | solution.py:12
  109.9 1.3 collective-permute-start.11
  111.2 1.1 convolution_dynamic-update-slice_fusion
  112.3 4.1 %collective-permute-done.11 = bf16[6,1,32,128]{3,2,1,0:T(8,128)(2,1)S(1)} collective-permute-done((bf16[6,1,32,128]{3,2,1,0:T(8,128)(2,1)S(1)}, bf16[6,1,32,128]{3,2,1,0:T(8,128)(2,1)S(1)}, u32[]{:S(2)}, u32[]{:S(2)}) %collective-permute-start.11) | collective-permute-done | bytes 49184 | tf_op jit(solution)/shard_map/ppermute | solution.py:15
  128.5 117.8 %all-reduce.8.cloned.1.call-done = (f32[27,64,128]{2,1,0:T(8,128)}, f32[27,128,128]{2,1,0:T(8,128)}) async-done(((f32[27,64,128]{2,1,0:T(8,128)}, f32[27,128,128]{2,1,0:T(8,128)}), (f32[27,64,128]{2,1,0:T(8,128)}, f32[27,128,128]{2,1,0:T(8,128)})) %all-reduce.8.cloned.1.call-update) | async-done | bytes 2654224 | tf_op jit(solution)/shard_map/psum | solution.py:101
  246.4 61.9 %all-reduce.10.cloned.1.call-done = (f32[27,64,128]{2,1,0:T(8,128)}, f32[27,128,128]{2,1,0:T(8,128)}) async-done(((f32[27,64,128]{2,1,0:T(8,128)}, f32[27,128,128]{2,1,0:T(8,128)}), (f32[27,64,128]{2,1,0:T(8,128)}, f32[27,128,128]{2,1,0:T(8,128)})) %all-reduce.10.cloned.1.call-update) | async-done | bytes 2654224 | tf_op jit(solution)/shard_map/psum | solution.py:101
  308.3 2.7 multiply_reduce_fusion
  311.7 1.3 broadcast_multiply_fusion
  (229 shorter events, 42.0 us)
Async XLA Ops:
  7.2 7.8 %copy-start.37 = (bf16[4,8,16,128]{3,2,1,0:T(8,128)(2,1)S(1)}, bf16[4,8,16,128]{3,2,1,0:T(8,128)(2,1)}, u32[]{:S(2)}) copy-start(bf16[4,8,16,128]{3,2,1,0:T(8,128)(2,1)} %param.7) | copy-start | bytes 393220
  7.2 7.2 %copy-start.38 = (bf16[27,64,128]{2,1,0:T(8,128)(2,1)S(1)}, bf16[27,64,128]{2,1,0:T(8,128)(2,1)}, u32[]{:S(2)}) copy-start(bf16[27,64,128]{2,1,0:T(8,128)(2,1)} %param.9) | copy-start | bytes 1327108
  7.2 239.1 %all-reduce.8.cloned.1.call-start = ((), (), s32[]{:S(2)}) async-start(), calls=%async_computation | async-start | bytes 5308416 | tf_op jit(solution)/shard_map/psum | solution.py:101
  8.2 8.3 %collective-permute-start = (bf16[1,8,32,64]{3,2,1,0:T(8,128)(2,1)S(1)}, bf16[1,8,32,64]{3,2,1,0:T(8,128)(2,1)S(1)}, u32[]{:S(2)}, u32[]{:S(2)}) collective-permute-start(bf16[1,8,32,64]{3,2,1,0:T(8,128)(2,1)S(1)} %slice.487), channel_id=1, source_target_pairs={{0,8},{8,16},{16,24},{1,9},{9,17},{17,25},{2,10},{10,18},{18,26},{... | collective-permute-start | bytes 98312 | tf_op jit(solution)/shard_map/ppermute | solution.py:12
  10.6 4.6 %copy-start.4 = (bf16[27,128,128]{2,1,0:T(8,128)(2,1)S(1)}, bf16[27,128,128]{2,1,0:T(8,128)(2,1)}, u32[]{:S(2)}) copy-start(bf16[27,128,128]{2,1,0:T(8,128)(2,1)} %param.11) | copy-start | bytes 2654212
  10.7 5.9 %collective-permute-start.1 = (bf16[1,8,32,64]{3,2,1,0:T(8,128)(2,1)S(1)}, bf16[1,8,32,64]{3,2,1,0:T(8,128)(2,1)S(1)}, u32[]{:S(2)}, u32[]{:S(2)}) collective-permute-start(bf16[1,8,32,64]{3,2,1,0:T(8,128)(2,1)S(1)} %slice.489), channel_id=1, source_target_pairs={{8,0},{16,8},{24,16},{9,1},{17,9},{25,17},{10,2},{18,10},{26,18},{... | collective-permute-start | bytes 98312 | tf_op jit(solution)/shard_map/ppermute | solution.py:15
  16.5 6.8 %copy-start.58 = (s32[4,8,32]{2,1,0:T(8,128)S(1)}, s32[4,8,32]{2,1,0:T(8,128)}, u32[]{:S(2)}) copy-start(s32[4,8,32]{2,1,0:T(8,128)} %param.8) | copy-start | bytes 12292
  16.6 7.4 %collective-permute-start.2 = (bf16[6,1,32,64]{3,2,1,0:T(8,128)(2,1)S(1)}, bf16[6,1,32,64]{3,2,1,0:T(8,128)(2,1)S(1)}, u32[]{:S(2)}, u32[]{:S(2)}) collective-permute-start(bf16[6,1,32,64]{3,2,1,0:T(8,128)(2,1)S(1)} %get-tuple-element.118), channel_id=1, source_target_pairs={{0,1},{1,2},{2,3},{3,4},{4,5},{5,6},{6,7},{8,9},{9,10},{10,11},{11... | collective-permute-start | bytes 73736 | tf_op jit(solution)/shard_map/ppermute | solution.py:12
  20.9 6.0 %collective-permute-start.3 = (bf16[6,1,32,64]{3,2,1,0:T(8,128)(2,1)S(1)}, bf16[6,1,32,64]{3,2,1,0:T(8,128)(2,1)S(1)}, u32[]{:S(2)}, u32[]{:S(2)}) collective-permute-start(bf16[6,1,32,64]{3,2,1,0:T(8,128)(2,1)S(1)} %get-tuple-element.119), channel_id=1, source_target_pairs={{1,0},{2,1},{3,2},{4,3},{5,4},{6,5},{7,6},{9,8},{10,9},{11,10},{12... | collective-permute-start | bytes 73736 | tf_op jit(solution)/shard_map/ppermute | solution.py:15
  23.3 8.1 %copy-start.15 = (bf16[1024,64]{1,0:T(8,128)(2,1)}, bf16[1024,64]{1,0:T(8,128)(2,1)S(1)}, u32[]{:S(2)}) copy-start(bf16[1024,64]{1,0:T(8,128)(2,1)S(1)} %concatenate.198) | copy-start | bytes 393220
  28.4 1.3 copy-start.3
  29.7 3.0 copy-start.17
  32.9 5.5 %copy-start.5 = (bf16[27,128,128]{2,1,0:T(8,128)(2,1)S(1)}, bf16[27,128,128]{2,1,0:T(8,128)(2,1)}, u32[]{:S(2)}) copy-start(bf16[27,128,128]{2,1,0:T(8,128)(2,1)} %reverse_bitcast_fusion) | copy-start | bytes 2654212
  34.0 15.9 %copy-start.16 = (bf16[1024,64]{1,0:T(8,128)(2,1)S(1)}, bf16[1024,64]{1,0:T(8,128)(2,1)}, u32[]{:S(2)}) copy-start(bf16[1024,64]{1,0:T(8,128)(2,1)} %copy-done.15) | copy-start | bytes 393220
  34.0 5.3 %collective-permute-start.4 = (bf16[1,8,32,128]{3,2,1,0:T(8,128)(2,1)S(1)}, bf16[1,8,32,128]{3,2,1,0:T(8,128)(2,1)S(1)}, u32[]{:S(2)}, u32[]{:S(2)}) collective-permute-start(bf16[1,8,32,128]{3,2,1,0:T(8,128)(2,1)S(1)} %bitcast.334), channel_id=1, source_target_pairs={{0,8},{8,16},{16,24},{1,9},{9,17},{17,25},{2,10},{10,18},{18,26},{... | collective-permute-start | bytes 196616 | tf_op jit(solution)/shard_map/ppermute | solution.py:12
  37.1 5.8 %collective-permute-start.5 = (bf16[1,8,32,128]{3,2,1,0:T(8,128)(2,1)S(1)}, bf16[1,8,32,128]{3,2,1,0:T(8,128)(2,1)S(1)}, u32[]{:S(2)}, u32[]{:S(2)}) collective-permute-start(bf16[1,8,32,128]{3,2,1,0:T(8,128)(2,1)S(1)} %bitcast.333), channel_id=1, source_target_pairs={{8,0},{16,8},{24,16},{9,1},{17,9},{25,17},{10,2},{18,10},{26,18},{... | collective-permute-start | bytes 196616 | tf_op jit(solution)/shard_map/ppermute | solution.py:15
  43.5 17.1 %collective-permute-start.6 = (bf16[6,1,32,128]{3,2,1,0:T(8,128)(2,1)}, bf16[6,1,32,128]{3,2,1,0:T(8,128)(2,1)}, u32[]{:S(2)}, u32[]{:S(2)}) collective-permute-start(bf16[6,1,32,128]{3,2,1,0:T(8,128)(2,1)} %get-tuple-element.112), channel_id=1, source_target_pairs={{0,1},{1,2},{2,3},{3,4},{4,5},{5,6},{6,7},{8,9},{9,10},{10,11},{11... | collective-permute-start | bytes 147464 | tf_op jit(solution)/shard_map/ppermute | solution.py:12
  48.5 12.2 %collective-permute-start.7 = (bf16[6,1,32,128]{3,2,1,0:T(8,128)(2,1)}, bf16[6,1,32,128]{3,2,1,0:T(8,128)(2,1)}, u32[]{:S(2)}, u32[]{:S(2)}) collective-permute-start(bf16[6,1,32,128]{3,2,1,0:T(8,128)(2,1)} %get-tuple-element.113), channel_id=1, source_target_pairs={{1,0},{2,1},{3,2},{4,3},{5,4},{6,5},{7,6},{9,8},{10,9},{11,10},{12... | collective-permute-start | bytes 147464 | tf_op jit(solution)/shard_map/ppermute | solution.py:15
  54.0 1.9 copy-start.19
  56.9 2.8 copy-start.18
  70.7 1.3 copy-start.2
  71.9 1.3 copy-start.34
  74.3 1.2 copy-start.36
  79.3 4.1 %copy-start.49 = (bf16[3,128,128]{2,1,0:T(8,128)(2,1)S(1)}, bf16[3,128,128]{2,1,0:T(8,128)(2,1)}, u32[]{:S(2)}) copy-start(bf16[3,128,128]{2,1,0:T(8,128)(2,1)} %get-tuple-element.22) | copy-start | bytes 294916
  81.6 2.1 copy-start.48
  85.4 1.1 copy-start.1
  85.4 1.1 copy-start.43
  85.9 1.2 copy-start.35
  87.5 1.9 copy-start.7
  88.8 9.1 %copy-start.8 = (bf16[1024,384]{0,1:T(8,128)(2,1)S(1)}, bf16[1024,384]{0,1:T(8,128)(2,1)}, u32[]{:S(2)}) copy-start(bf16[1024,384]{0,1:T(8,128)(2,1)} %copy.41) | copy-start | bytes 2359300
  90.5 8.5 %copy-start.9 = (bf16[1024,384]{0,1:T(8,128)(2,1)S(1)}, bf16[1024,384]{0,1:T(8,128)(2,1)}, u32[]{:S(2)}) copy-start(bf16[1024,384]{0,1:T(8,128)(2,1)} %copy.42) | copy-start | bytes 2359300
  91.7 8.4 %copy-start.11 = (bf16[1024,384]{0,1:T(8,128)(2,1)S(1)}, bf16[1024,384]{0,1:T(8,128)(2,1)}, u32[]{:S(2)}) copy-start(bf16[1024,384]{0,1:T(8,128)(2,1)} %copy.43) | copy-start | bytes 2359300
  91.7 13.9 %collective-permute-start.8 = (bf16[1,8,32,128]{3,2,1,0:T(8,128)(2,1)}, bf16[1,8,32,128]{3,2,1,0:T(8,128)(2,1)S(1)}, u32[]{:S(2)}, u32[]{:S(2)}) collective-permute-start(bf16[1,8,32,128]{3,2,1,0:T(8,128)(2,1)} %bitcast.45), channel_id=1, source_target_pairs={{0,8},{8,16},{16,24},{1,9},{9,17},{17,25},{2,10},{10,18},{18,26},{... | collective-permute-start | bytes 196616 | tf_op jit(solution)/shard_map/ppermute | solution.py:12
  96.4 9.2 %collective-permute-start.9 = (bf16[1,8,32,128]{3,2,1,0:T(8,128)(2,1)}, bf16[1,8,32,128]{3,2,1,0:T(8,128)(2,1)S(1)}, u32[]{:S(2)}, u32[]{:S(2)}) collective-permute-start(bf16[1,8,32,128]{3,2,1,0:T(8,128)(2,1)} %bitcast.332), channel_id=1, source_target_pairs={{8,0},{16,8},{24,16},{9,1},{17,9},{25,17},{10,2},{18,10},{26,18},{... | collective-permute-start | bytes 196616 | tf_op jit(solution)/shard_map/ppermute | solution.py:15
  97.9 3.2 copy-start.14
  99.0 3.2 copy-start.10
  100.0 3.2 copy-start.13
  101.1 3.2 copy-start.12
  105.6 6.6 %collective-permute-start.10 = (bf16[6,1,32,128]{3,2,1,0:T(8,128)(2,1)S(1)}, bf16[6,1,32,128]{3,2,1,0:T(8,128)(2,1)S(1)}, u32[]{:S(2)}, u32[]{:S(2)}) collective-permute-start(bf16[6,1,32,128]{3,2,1,0:T(8,128)(2,1)S(1)} %get-tuple-element.108), channel_id=1, source_target_pairs={{0,1},{1,2},{2,3},{3,4},{4,5},{5,6},{6,7},{8,9},{9,10},{10,11},{11... | collective-permute-start | bytes 147464 | tf_op jit(solution)/shard_map/ppermute | solution.py:12
  109.9 6.4 %collective-permute-start.11 = (bf16[6,1,32,128]{3,2,1,0:T(8,128)(2,1)S(1)}, bf16[6,1,32,128]{3,2,1,0:T(8,128)(2,1)S(1)}, u32[]{:S(2)}, u32[]{:S(2)}) collective-permute-start(bf16[6,1,32,128]{3,2,1,0:T(8,128)(2,1)S(1)} %get-tuple-element.109), channel_id=1, source_target_pairs={{1,0},{2,1},{3,2},{4,3},{5,4},{6,5},{7,6},{9,8},{10,9},{11,10},{12... | collective-permute-start | bytes 147464 | tf_op jit(solution)/shard_map/ppermute | solution.py:15
  124.1 1.3 copy-start.28
  124.6 1.3 copy-start.25
  124.6 1.6 copy-start.24
  125.3 1.1 copy-start.23
  125.6 1.1 copy-start.22
  128.5 179.8 %all-reduce.10.cloned.1.call-start = ((), (), s32[]{:S(2)}) async-start(), calls=%async_computation.1 | async-start | bytes 5308416 | tf_op jit(solution)/shard_map/psum | solution.py:101
  308.3 3.4 %copy-start = (f32[27,128,128]{2,1,0:T(8,128)S(1)}, f32[27,128,128]{2,1,0:T(8,128)}, u32[]{:S(2)}) copy-start(f32[27,128,128]{2,1,0:T(8,128)} %get-tuple-element.6) | copy-start | bytes 5308420
  311.7 1.5 copy-start.6
  (30 other events, 28.7 us)
Sparse Core Ops, SparseCore 0:
  128.6 117.6 all-reduce.7
  248.7 59.4 all-reduce.9
